TPU v7x, 256 devices: a whole 4x4x8 slice. The times are simulated.
256 devices in a mesh: expert: 64 (over y, z, core), tensor: 4 (over x).
Axes of the slice: x: 4, y: 4, z: 8, core: 2. Of those that a mesh axis runs over, the one named last changes fastest.
Arguments:
- attn_heads: bfloat16 [8192, 4096], P('expert', 'tensor'), may hold values from -6 to 6
- out_proj: bfloat16 [4096, 4096], P('tensor', 'expert'), may hold values from -0.09375 to 0.09375
- residual: bfloat16 [8192, 4096], P('expert'), may hold values from -6 to 6
- norm_gain: float32 [4096], replicated, may hold values from 0.1 to 1.9
- route_ids: int32 [8192, 8], P('expert'), may hold values from 0 to 63, all different within a row; in each aligned block of 128 rows (0 to 127, 128 to 255, ...) at most 18 rows name the same one
- route_weights: float32 [8192, 8], P('expert'), may hold values from 0.05 to 1
- w_gate: bfloat16 [64, 4096, 1536], P('expert', None, 'tensor'), may hold values from -0.09375 to 0.09375
- w_up: bfloat16 [64, 4096, 1536], P('expert', None, 'tensor'), may hold values from -0.09375 to 0.09375
- w_down: bfloat16 [64, 1536, 4096], P('expert', 'tensor'), may hold values from -0.15625 to 0.15625
Outputs:
- layer_out: bfloat16 [8192, 4096], P('expert', 'tensor')
Inputs may be any that keep to these rules, and one draw needn't show every extreme that they name: `route_ids`: each row names 8 different experts. In aligned blocks of 128 rows no expert is named more than 18 times, a bound that some block reaches.
All inputs are finite; a program needn't handle non-finite values.
Results may differ from a plain program's by a relative error of at most 0.015.
Values may be sent and summed in bfloat16 or wider, within the bound.
A program may use at most 128 MiB of HBM per device.

v0:
```python
import jax
import jax.numpy as jnp
from jax import lax
from jax.sharding import PartitionSpec as P

EXPERTS = 64
MAIN = 16
OVER = 2
LANES = 128


def routing(route_ids, route_weights):
    count = route_ids.shape[0]
    hits = (route_ids[:, :, None] == jnp.arange(EXPERTS, dtype=jnp.int32)[None, None, :]).astype(
        jnp.float32
    )
    chosen = jnp.sum(hits, axis=1)
    weights = route_weights / jnp.sum(route_weights, axis=-1, keepdims=True)
    weight = jnp.sum(hits * weights[:, :, None], axis=1)
    order = jnp.arange(count, dtype=jnp.int32)
    earlier = (order[None, :] < order[:, None]).astype(jnp.bfloat16)
    rank = jnp.dot(earlier, chosen.astype(jnp.bfloat16), preferred_element_type=jnp.float32)
    rank = jnp.where(chosen > 0, rank, -1.0)
    return (rank.astype(jnp.int32), weight)


def per_device(
    attn_heads, out_proj, residual, norm_gain, route_ids, route_weights, w_gate, w_up, w_down
):
    tokens, model_width = residual.shape
    members = lax.axis_size("tensor")
    member = lax.axis_index("tensor")
    cols = model_width // members
    groups = cols // LANES
    rows = EXPERTS * MAIN
    rank, weight = routing(route_ids, route_weights)
    row = jnp.arange(rows, dtype=jnp.int32)
    slot = row % MAIN
    spread = jnp.repeat(rank, MAIN, axis=1)
    main_hit = spread == slot[None, :]
    over_hit = spread == (MAIN + slot // groups)[None, :]
    row_weight = jnp.repeat(weight, MAIN, axis=1)
    heads_out = jnp.dot(
        attn_heads,
        lax.all_gather(out_proj, "expert", axis=1, tiled=True),
        preferred_element_type=jnp.float32,
    ).astype(jnp.bfloat16)
    attn_out = lax.psum_scatter(
        jnp.transpose(heads_out.reshape(tokens, members, cols), (1, 0, 2)),
        "tensor",
        scatter_dimension=0,
        tiled=True,
    )[0].astype(jnp.float32)
    own_residual = lax.dynamic_slice_in_dim(residual, member * cols, cols, 1)
    own_gain = lax.dynamic_slice_in_dim(norm_gain, member * cols, cols, 0)
    hidden = own_residual.astype(jnp.float32) + attn_out
    squares = lax.psum(jnp.sum(hidden * hidden, axis=-1, keepdims=True), "tensor")
    normed = (hidden * lax.rsqrt(squares / model_width + 1e-06) * own_gain).astype(jnp.bfloat16)
    main = jnp.einsum(
        "tr,td->rd", main_hit.astype(jnp.bfloat16), normed, preferred_element_type=jnp.float32
    ).astype(jnp.bfloat16)
    wide = jnp.einsum(
        "tr,td->rd", over_hit.astype(jnp.bfloat16), normed, preferred_element_type=jnp.float32
    ).astype(jnp.bfloat16)
    own_group = (row % groups)[:, None]
    over = jnp.zeros((rows, LANES), jnp.bfloat16)
    for g in range(groups):
        over = jnp.where(own_group == g, wide[:, g * LANES : (g + 1) * LANES], over)
    packed = jnp.concatenate([main, over], axis=1).reshape(EXPERTS, MAIN, cols + LANES)
    arrived = lax.all_to_all(packed, "expert", split_axis=0, concat_axis=0, tiled=True)
    full = lax.all_gather(arrived.reshape(rows, cols + LANES), "tensor", axis=0)
    main_in = jnp.concatenate([full[m, :, :cols] for m in range(members)], axis=1)
    over_in = jnp.transpose(
        full[:, :, cols:].reshape(members, EXPERTS * OVER, groups, LANES), (1, 0, 2, 3)
    ).reshape(EXPERTS * OVER, model_width)
    inputs = jnp.concatenate([main_in, over_in], axis=0)
    gate = jnp.dot(inputs, w_gate[0], preferred_element_type=jnp.float32)
    up = jnp.dot(inputs, w_up[0], preferred_element_type=jnp.float32)
    act = (jax.nn.silu(gate) * up).astype(jnp.bfloat16)
    down = w_down[0].reshape(-1, members, cols)
    parts = jnp.stack(
        [jnp.dot(act, down[:, m], preferred_element_type=jnp.float32) for m in range(members)]
    ).astype(jnp.bfloat16)
    summed = lax.psum_scatter(parts, "tensor", scatter_dimension=0, tiled=True)[0]
    back = jnp.concatenate([summed[:rows], summed[rows:].reshape(rows, LANES)], axis=1).reshape(
        EXPERTS, MAIN, cols + LANES
    )
    returned = lax.all_to_all(back, "expert", split_axis=0, concat_axis=0, tiled=True).reshape(
        rows, cols + LANES
    )
    high = row_weight.astype(jnp.bfloat16)
    low = (row_weight - high.astype(jnp.float32)).astype(jnp.bfloat16)
    mixture = 0.0
    zero = jnp.zeros((), jnp.bfloat16)
    for part in (high, low):
        pick = jnp.where(main_hit, part, zero)
        mixture += jnp.dot(pick, returned[:, :cols], preferred_element_type=jnp.float32)
        extra = [
            jnp.dot(
                jnp.where(over_hit & (row % groups == g)[None, :], part, zero),
                returned[:, cols:],
                preferred_element_type=jnp.float32,
            )
            for g in range(groups)
        ]
        mixture += jnp.concatenate(extra, axis=1)
    return (hidden + mixture).astype(jnp.bfloat16)


def solution(mesh):
    placed = (
        P("expert", "tensor"),
        P("tensor", "expert"),
        P("expert", None),
        P(),
        P("expert", None),
        P("expert", None),
        P("expert", None, "tensor"),
        P("expert", None, "tensor"),
        P("expert", "tensor", None),
    )
    return jax.shard_map(
        per_device, mesh=mesh, in_specs=placed, out_specs=P("expert", "tensor"), check_vma=False
    )
```

profile of v0, /device:TPU:1, one launch (start us, length us, event | category | flops | bytes accessed | tf_op | source)
XLA Modules:
  0.0 545.0 jit_solution(5907444600638670567)
XLA Ops:
  7.3 90.1 %all-gather.3.cloned.1.call-done = bf16[1024,4096]{0,1:T(8,128)(2,1)} async-done(((bf16[1024,64]{0,1:T(8,128)(2,1)}), bf16[1024,4096]{0,1:T(8,128)(2,1)}) %all-gather.3.cloned.1.call-update) | async-done | bytes 8388624 | tf_op jit(solution)/shard_map/all_gather | solution.py:45
  97.5 6.3 %convolution_convert_fusion = bf16[128,4096]{1,0:T(8,128)(2,1)S(1)} fusion(bf16[128,1024]{1,0:T(8,128)(2,1)} %param.9, bf16[1024,4096]{0,1:T(8,128)(2,1)} %all-gather.3.cloned.1.call-done), kind=kOutput, calls=%fused_computation.2 | convolution fusion | flops 1074266112 | bytes 9699328 | tf_op jit(solution)/shard_map/dot_general | solution.py:43
  107.1 1.3 bitcast_compare_fusion.1
  110.8 15.7 %reduce-scatter.3.cloned.1.call-done = bf16[1,128,1024]{2,1,0:T(8,128)(2,1)} async-done(((bf16[4,128,1024]{2,1,0:T(8,128)(2,1)}), bf16[1,128,1024]{2,1,0:T(8,128)(2,1)}) %reduce-scatter.3.cloned.1.call-update) | async-done | bytes 262160 | tf_op jit(solution)/shard_map/reduce_scatter | solution.py:48
  126.5 1.2 multiply_reduce_fusion
  127.7 6.5 %psum.7 = f32[128,1]{0,1:T(1,128)S(1)} all-reduce(f32[128,1]{0,1:T(1,128)S(1)} %bitcast.221), channel_id=1, replica_groups=mesh['expert'=64,'tensor'=4] {'tensor'}, use_global_device_ids=true, to_apply=%region_5.6 | all-reduce | flops 128 | bytes 1024 | tf_op jit(solution)/shard_map/psum | solution.py:57
  134.3 2.0 convolution_convert_fusion.5
  136.6 1.8 convolution_convert_fusion.6
  138.3 1.7 pad_maximum_fusion.2
  140.0 4.4 copy.131
  144.3 71.2 %all_to_all.10 = bf16[64,16,1152]{2,1,0:T(8,128)(2,1)} all-to-all(bf16[64,16,1152]{2,1,0:T(8,128)(2,1)} %bitcast.212), channel_id=1, replica_groups=mesh['expert'=64,'tensor'=4] {'expert'}, dimensions={0} | all-to-all | bytes 4718592 | tf_op jit(solution)/shard_map/all_to_all | solution.py:70
  215.8 4.7 copy.134
  220.5 84.6 %all-gather.5.cloned.1.call-done = bf16[4,1024,1152]{2,1,0:T(8,128)(2,1)} async-done(((bf16[1,1024,1152]{2,1,0:T(8,128)(2,1)}), bf16[4,1024,1152]{2,1,0:T(8,128)(2,1)}) %all-gather.5.cloned.1.call-update) | async-done | bytes 9437200 | tf_op jit(solution)/shard_map/all_gather | solution.py:71
  305.1 2.3 slice_bitcast_fusion.4
  307.3 2.4 copy.132
  309.8 2.3 copy.133
  312.1 4.9 slice_bitcast_fusion.3
  317.0 19.2 %fusion.5 = f32[1152,384]{1,0:T(8,128)} fusion(bf16[1,4096,384]{2,1,0:T(8,128)(2,1)S(1)} %copy-done, bf16[128,4096]{1,0:T(8,128)(2,1)S(1)} %copy-done.19, bf16[1024,1024]{1,0:T(8,128)(2,1)S(1)} %get-tuple-element.8, bf16[1024,1024]{1,0:T(8,128)(2,1)S(1)} %get-tuple-element.9, bf16[1024,1024]{1,0:T(8,128)(2,1)} %get-tuple-element.10, ...), kind=kOutput, calls=%fused_computation.13 | convolution fusion | flops 3671064576 | bytes 14352384 | tf_op jit(solution)/shard_map/dot_general | solution.py:77
  336.3 16.9 %fusion.7 = bf16[1152,384]{1,0:T(8,128)(2,1)} fusion(bf16[1,4096,384]{2,1,0:T(8,128)(2,1)} %param.16, f32[1152,384]{1,0:T(8,128)} %fusion.5, bf16[128,4096]{1,0:T(8,128)(2,1)S(1)} %copy-done.19, bf16[1024,1024]{1,0:T(8,128)(2,1)S(1)} %get-tuple-element.8, bf16[1024,1024]{1,0:T(8,128)(2,1)S(1)} %get-tuple-element.9, ...), kind=kOutput, calls=%fused_computation.15 | convolution fusion | flops 3673718784 | bytes 15237120 | tf_op jit(solution)/shard_map/dot_general | solution.py:78
  353.2 2.7 fusion.3
  355.8 1.4 fusion.2
  357.3 1.4 fusion.1
  358.7 1.4 fusion
  360.1 4.6 pad_maximum_fusion.1
  364.7 92.7 %reduce-scatter.5.cloned.1.call-done = bf16[1,1152,1024]{2,1,0:T(8,128)(2,1)} async-done(((bf16[4,1152,1024]{2,1,0:T(8,128)(2,1)}), bf16[1,1152,1024]{2,1,0:T(8,128)(2,1)}) %reduce-scatter.5.cloned.1.call-update) | async-done | bytes 2359312 | tf_op jit(solution)/shard_map/reduce_scatter | solution.py:84
  458.5 1.5 slice-done
  460.0 1.7 pad_maximum_fusion.3
  461.7 10.6 %all-to-all-start.1 = ((bf16[64,16,1152]{2,1,0:T(8,128)(2,1)}), bf16[64,16,1152]{2,1,0:T(8,128)(2,1)S(1)}, u32[]{:S(2)}, u32[]{:S(2)}) async-start(bf16[64,16,1152]{2,1,0:T(8,128)(2,1)} %pad_maximum_fusion.3), calls=%async_computation.3 | async-start | bytes 4718592 | tf_op jit(solution)/shard_map/all_to_all | solution.py:88
  472.5 4.6 fusion.39
  477.1 51.9 %all-to-all-done.1 = bf16[64,16,1152]{2,1,0:T(8,128)(2,1)S(1)} async-done(((bf16[64,16,1152]{2,1,0:T(8,128)(2,1)}), bf16[64,16,1152]{2,1,0:T(8,128)(2,1)S(1)}, u32[]{:S(2)}, u32[]{:S(2)}) %all-to-all-start.1) | async-done | bytes 2359328 | tf_op jit(solution)/shard_map/all_to_all | solution.py:88
  529.1 1.7 fusion.10
  535.5 3.0 fusion.26
  (120 shorter events, 12.4 us)
Async XLA Ops:
  6.5 310.5 %copy-start = (bf16[1,4096,384]{2,1,0:T(8,128)(2,1)S(1)}, bf16[1,4096,384]{2,1,0:T(8,128)(2,1)}, u32[]{:S(2)}) copy-start(bf16[1,4096,384]{2,1,0:T(8,128)(2,1)} %param.15) | copy-start | bytes 9437188
  6.5 90.9 %all-gather.3.cloned.1.call-start = ((), (), s32[]{:S(2)}) async-start(), calls=%async_computation.4 | async-start | bytes 8519680 | tf_op jit(solution)/shard_map/all_gather | solution.py:45
  7.3 119.3 %reduce-scatter.3.cloned.1.call-start = ((), (), s32[]{:S(2)}) async-start(), calls=%async_computation.5 | async-start | bytes 1310720 | tf_op jit(solution)/shard_map/reduce_scatter | solution.py:48
  104.9 200.2 %all-gather.5.cloned.1.call-start = ((), (), s32[]{:S(2)}) async-start(), calls=%async_computation.6 | async-start | bytes 11796480 | tf_op jit(solution)/shard_map/all_gather | solution.py:71
  134.3 2.3 copy-start.3
  215.5 241.9 %reduce-scatter.5.cloned.1.call-start = ((), (), s32[]{:S(2)}) async-start(), calls=%async_computation.7 | async-start | bytes 11796480 | tf_op jit(solution)/shard_map/reduce_scatter | solution.py:84
  312.1 5.0 copy-start.19
  336.3 16.9 %copy-start.4 = (bf16[1,384,4096]{1,2,0:T(8,128)(2,1)S(1)}, bf16[1,384,4096]{1,2,0:T(8,128)(2,1)}, u32[]{:S(2)}) copy-start(bf16[1,384,4096]{1,2,0:T(8,128)(2,1)} %copy.134) | copy-start | bytes 9437188
  353.1 2.7 copy-start.39
  461.7 10.7 %copy-start.20 = (f32[128,64]{0,1:T(8,128)S(1)}, f32[128,64]{0,1:T(8,128)}, u32[]{:S(2)}) copy-start(f32[128,64]{0,1:T(8,128)} %get-tuple-element.6) | copy-start | bytes 98308
  461.7 10.7 %copy-start.22 = (s32[128,64]{0,1:T(8,128)S(1)}, s32[128,64]{0,1:T(8,128)}, u32[]{:S(2)}) copy-start(s32[128,64]{0,1:T(8,128)} %copy-done.21) | copy-start | bytes 98308
  461.7 10.7 %copy-start.25 = (pred[1024]{0:T(1024)(128)(4,1)S(1)}, pred[1024]{0:T(1024)(128)(4,1)}, u32[]{:S(2)}) copy-start(pred[1024]{0:T(1024)(128)(4,1)} %get-tuple-element.70) | copy-start | bytes 3076
  461.7 10.7 %copy-start.27 = (pred[1024]{0:T(1024)(128)(4,1)S(1)}, pred[1024]{0:T(1024)(128)(4,1)}, u32[]{:S(2)}) copy-start(pred[1024]{0:T(1024)(128)(4,1)} %get-tuple-element.67) | copy-start | bytes 3076
  461.7 10.7 %copy-start.29 = (pred[1024]{0:T(1024)(128)(4,1)S(1)}, pred[1024]{0:T(1024)(128)(4,1)}, u32[]{:S(2)}) copy-start(pred[1024]{0:T(1024)(128)(4,1)} %get-tuple-element.68) | copy-start | bytes 3076
  461.7 10.7 %copy-start.31 = (pred[1024]{0:T(1024)(128)(4,1)S(1)}, pred[1024]{0:T(1024)(128)(4,1)}, u32[]{:S(2)}) copy-start(pred[1024]{0:T(1024)(128)(4,1)} %get-tuple-element.65) | copy-start | bytes 3076
  461.7 10.7 %copy-start.33 = (pred[1024]{0:T(1024)(128)(4,1)S(1)}, pred[1024]{0:T(1024)(128)(4,1)}, u32[]{:S(2)}) copy-start(pred[1024]{0:T(1024)(128)(4,1)} %get-tuple-element.66) | copy-start | bytes 3076
  461.7 10.7 %copy-start.35 = (pred[1024]{0:T(1024)(128)(4,1)S(1)}, pred[1024]{0:T(1024)(128)(4,1)}, u32[]{:S(2)}) copy-start(pred[1024]{0:T(1024)(128)(4,1)} %get-tuple-element.63) | copy-start | bytes 3076
  461.7 10.7 %copy-start.37 = (pred[1024]{0:T(1024)(128)(4,1)S(1)}, pred[1024]{0:T(1024)(128)(4,1)}, u32[]{:S(2)}) copy-start(pred[1024]{0:T(1024)(128)(4,1)} %get-tuple-element.64) | copy-start | bytes 3076
  461.7 67.3 %all-to-all-start.1 = ((bf16[64,16,1152]{2,1,0:T(8,128)(2,1)}), bf16[64,16,1152]{2,1,0:T(8,128)(2,1)S(1)}, u32[]{:S(2)}, u32[]{:S(2)}) async-start(bf16[64,16,1152]{2,1,0:T(8,128)(2,1)} %pad_maximum_fusion.3), calls=%async_computation.3 | async-start | bytes 4718592 | tf_op jit(solution)/shard_map/all_to_all | solution.py:88
  529.0 6.1 %copy-start.2 = (bf16[64,16,1152]{2,1,0:T(8,128)(2,1)}, bf16[64,16,1152]{2,1,0:T(8,128)(2,1)S(1)}, u32[]{:S(2)}) copy-start(bf16[64,16,1152]{2,1,0:T(8,128)(2,1)S(1)} %all-to-all-done.1) | copy-start | bytes 7077892
  529.0 2.1 copy-start.17
  529.0 2.4 copy-start.16
  529.1 2.7 copy-start.15
  529.1 3.0 copy-start.14
  529.1 3.3 copy-start.13
  530.9 2.3 copy-start.10
  531.2 2.3 copy-start.9
  531.5 2.3 copy-start.8
  531.7 2.3 copy-start.7
  532.0 2.3 copy-start.6
  533.2 2.3 copy-start.5
  535.5 3.0 copy-start.1
  (14 other events, 25.3 us)
Sparse Core Ops, SparseCore 0:
  10.1 87.2 all-gather.2
  105.0 21.4 reduce-scatter.2
  215.7 89.3 all-gather.4
  364.8 92.5 reduce-scatter.4
where the time goes:
time: 546 us; the launch traced here: 545 us
  waiting for transfers between devices  336 us (62%)
  blocking collectives  77.7 us (14%)
  matrix products  62.3 us (11%)
  local copies, waits for them, and re-layouts  26.1 us (5%)
  other arithmetic  18.2 us (3%)
  between operations  13.9 us (3%)
  starting transfers between devices  11 us (2%)
    reduce_scatter x1, waiting for transfers between devices, per_device(): lax.psum_scatter(parts, 'tensor', scatter_dimension=0, tiled=True)[0]  92.7 us
    all_gather x1, waiting for transfers between devices, per_device(): lax.all_gather(out_proj, 'expert', axis=1, tiled=True)  90.1 us
    all_gather x1, waiting for transfers between devices, per_device(): full = lax.all_gather(arrived.reshape(rows, cols + LANES), 'tensor', axis=0)  84.6 us
    all_to_all x1, blocking collectives, per_device(): lax.all_to_all(packed, 'expert', split_axis=0, concat_axis=0, tiled=True)  71.2 us
    all_to_all x1, waiting for transfers between devices, per_device(): lax.all_to_all(back, 'expert', split_axis=0, concat_axis=0, tiled=True)  51.9 us
    dot_general x1, matrix products, per_device(): gate = jnp.dot(inputs, w_gate[0], preferred_element_type=jnp.float32)  19.2 us
    dot_general x1, matrix products, per_device(): up = jnp.dot(inputs, w_up[0], preferred_element_type=jnp.float32)  16.9 us
    reduce_scatter x1, waiting for transfers between devices, per_device(): lax.psum_scatter(jnp.transpose(heads_out.reshape(tokens, members, cols),...  15.7 us
  transfers between devices with their start and end apart: 5, of which 5 were waited for; matrix products, arithmetic and copies ran while one was open for 3% of the time, Pallas kernels for 0%

commit v1 on v0

--- a/solution.py
+++ b/solution.py
@@ -7,6 +7,12 @@
 MAIN = 16
 OVER = 2
 LANES = 128
+
+
+def _place_files(buf):
+    return jnp.concatenate(
+        lax.all_to_all(jnp.stack(lax.axis_size("expert") * [buf], 0), "expert", 0, 0), 1
+    )
 
 
 def routing(route_ids, route_weights):
@@ -41,9 +47,7 @@
     over_hit = spread == (MAIN + slot // groups)[None, :]
     row_weight = jnp.repeat(weight, MAIN, axis=1)
     heads_out = jnp.dot(
-        attn_heads,
-        lax.all_gather(out_proj, "expert", axis=1, tiled=True),
-        preferred_element_type=jnp.float32,
+        attn_heads, _place_files(out_proj), preferred_element_type=jnp.float32
     ).astype(jnp.bfloat16)
     attn_out = lax.psum_scatter(
         jnp.transpose(heads_out.reshape(tokens, members, cols), (1, 0, 2)),

time: 546 us -> 653 us (1.20)
  blocking collectives: 77.7 us -> 277 us
  waiting for transfers between devices: 336 us -> 245 us
    all_to_all x0 -> x1, blocking collectives: none -> 199 us  [_place_files(): lax.all_to_all(jnp.stack(lax.axis_size('expert') * [buf], 0), 'expert', 0...]
    all_gather x1 -> x0, waiting for transfers between devices: 90.1 us -> none  [per_device(): lax.all_gather(out_proj, 'expert', axis=1, tiled=True)]
  transfers between devices with their start and end apart: 5 -> 4, of which waited for: 5 -> 4; matrix products, arithmetic and copies ran while one was open for 3% -> 2% of each run, Pallas kernels for 0% -> 0%
where the time goes in v1:
time: 653 us; the launch traced here: 652 us
  blocking collectives  277 us (42%)
  waiting for transfers between devices  245 us (38%)
  matrix products  59.7 us (9%)
  local copies, waits for them, and re-layouts  28.2 us (4%)
  other arithmetic  18.1 us (3%)
  between operations  13.8 us (2%)
  starting transfers between devices  10.9 us (2%)
    all_to_all x1, blocking collectives, _place_files(): lax.all_to_all(jnp.stack(lax.axis_size('expert') * [buf], 0), 'expert', 0...  199 us
    reduce_scatter x1, waiting for transfers between devices, per_device(): lax.psum_scatter(parts, 'tensor', scatter_dimension=0, tiled=True)[0]  92.7 us
    all_gather x1, waiting for transfers between devices, per_device(): full = lax.all_gather(arrived.reshape(rows, cols + LANES), 'tensor', axis=0)  84.6 us
    all_to_all x1, blocking collectives, per_device(): lax.all_to_all(packed, 'expert', split_axis=0, concat_axis=0, tiled=True)  71 us
    all_to_all x1, waiting for transfers between devices, per_device(): lax.all_to_all(back, 'expert', split_axis=0, concat_axis=0, tiled=True)  52 us
    dot_general x1, matrix products, per_device(): gate = jnp.dot(inputs, w_gate[0], preferred_element_type=jnp.float32)  19.2 us
    dot_general x1, matrix products, per_device(): up = jnp.dot(inputs, w_up[0], preferred_element_type=jnp.float32)  16.9 us
    reduce_scatter x1, waiting for transfers between devices, per_device(): lax.psum_scatter(jnp.transpose(heads_out.reshape(tokens, members, cols),...  15.4 us
  transfers between devices with their start and end apart: 4, of which 4 were waited for; matrix products, arithmetic and copies ran while one was open for 2% of the time, Pallas kernels for 0%

profile of v1, /device:TPU:1, one launch (start us, length us, event | category | flops | bytes accessed | tf_op | source)
XLA Modules:
  0.0 652.4 jit_solution(4091422079002573747)
XLA Ops:
  6.5 2.1 stack.17
  8.7 199.2 %all_to_all.15 = bf16[64,1024,64]{1,2,0:T(8,128)(2,1)S(1)} all-to-all(bf16[64,1024,64]{1,2,0:T(8,128)(2,1)S(1)} %stack.17), channel_id=1, replica_groups=mesh['expert'=64,'tensor'=4] {'expert'}, dimensions={0} | all-to-all | bytes 16777216 | tf_op jit(solution)/shard_map/all_to_all | solution.py:14
  207.8 2.8 convolution_convert_fusion
  217.7 15.4 %reduce-scatter.3.cloned.1.call-done = bf16[1,128,1024]{2,1,0:T(8,128)(2,1)} async-done(((bf16[4,128,1024]{2,1,0:T(8,128)(2,1)}), bf16[1,128,1024]{2,1,0:T(8,128)(2,1)}) %reduce-scatter.3.cloned.1.call-update) | async-done | bytes 262160 | tf_op jit(solution)/shard_map/reduce_scatter | solution.py:52
  234.3 6.7 %psum.7 = f32[128,1]{0,1:T(1,128)S(1)} all-reduce(f32[128,1]{0,1:T(1,128)S(1)} %bitcast.225), channel_id=1, replica_groups=mesh['expert'=64,'tensor'=4] {'tensor'}, use_global_device_ids=true, to_apply=%region_5.6 | all-reduce | flops 128 | bytes 1024 | tf_op jit(solution)/shard_map/psum | solution.py:61
  241.0 2.0 convolution_convert_fusion.5
  243.3 1.8 convolution_convert_fusion.6
  245.1 1.6 pad_maximum_fusion.2
  246.7 4.3 copy.132
  251.0 71.0 %all_to_all.16 = bf16[64,16,1152]{2,1,0:T(8,128)(2,1)} all-to-all(bf16[64,16,1152]{2,1,0:T(8,128)(2,1)} %bitcast.216), channel_id=1, replica_groups=mesh['expert'=64,'tensor'=4] {'expert'}, dimensions={0} | all-to-all | bytes 4718592 | tf_op jit(solution)/shard_map/all_to_all | solution.py:74
  322.3 4.7 copy.135
  326.9 84.6 %all-gather.2.cloned.1.call-done = bf16[4,1024,1152]{2,1,0:T(8,128)(2,1)} async-done(((bf16[1,1024,1152]{2,1,0:T(8,128)(2,1)}), bf16[4,1024,1152]{2,1,0:T(8,128)(2,1)}) %all-gather.2.cloned.1.call-update) | async-done | bytes 9437200 | tf_op jit(solution)/shard_map/all_gather | solution.py:75
  411.6 2.3 slice_bitcast_fusion.4
  413.9 2.4 copy.133
  416.3 2.3 copy.134
  418.5 5.0 slice_bitcast_fusion.3
  423.5 19.2 %fusion.5 = f32[1152,384]{1,0:T(8,128)} fusion(bf16[1,4096,384]{2,1,0:T(8,128)(2,1)S(1)} %copy-done, bf16[128,4096]{1,0:T(8,128)(2,1)S(1)} %copy-done.18, bf16[1024,1024]{1,0:T(8,128)(2,1)S(1)} %get-tuple-element.8, bf16[1024,1024]{1,0:T(8,128)(2,1)S(1)} %get-tuple-element.9, bf16[1024,1024]{1,0:T(8,128)(2,1)} %get-tuple-element.10, ...), kind=kOutput, calls=%fused_computation.13 | convolution fusion | flops 3671064576 | bytes 14352384 | tf_op jit(solution)/shard_map/dot_general | solution.py:81
  442.8 16.9 %fusion.7 = bf16[1152,384]{1,0:T(8,128)(2,1)} fusion(bf16[1,4096,384]{2,1,0:T(8,128)(2,1)} %param.16, f32[1152,384]{1,0:T(8,128)} %fusion.5, bf16[128,4096]{1,0:T(8,128)(2,1)S(1)} %copy-done.18, bf16[1024,1024]{1,0:T(8,128)(2,1)S(1)} %get-tuple-element.8, bf16[1024,1024]{1,0:T(8,128)(2,1)S(1)} %get-tuple-element.9, ...), kind=kOutput, calls=%fused_computation.15 | convolution fusion | flops 3673718784 | bytes 15237120 | tf_op jit(solution)/shard_map/dot_general | solution.py:82
  459.6 2.7 fusion
  462.3 1.4 fusion.1
  463.8 1.4 fusion.2
  465.2 1.4 fusion.3
  466.6 4.5 pad_maximum_fusion.1
  471.2 92.7 %reduce-scatter.5.cloned.1.call-done = bf16[1,1152,1024]{2,1,0:T(8,128)(2,1)} async-done(((bf16[4,1152,1024]{2,1,0:T(8,128)(2,1)}), bf16[1,1152,1024]{2,1,0:T(8,128)(2,1)}) %reduce-scatter.5.cloned.1.call-update) | async-done | bytes 2359312 | tf_op jit(solution)/shard_map/reduce_scatter | solution.py:88
  565.1 1.5 slice-done
  566.5 1.7 pad_maximum_fusion.3
  568.2 10.6 %all-to-all-start.2 = ((bf16[64,16,1152]{2,1,0:T(8,128)(2,1)}), bf16[64,16,1152]{2,1,0:T(8,128)(2,1)S(1)}, u32[]{:S(2)}, u32[]{:S(2)}) async-start(bf16[64,16,1152]{2,1,0:T(8,128)(2,1)} %pad_maximum_fusion.3), calls=%async_computation.4 | async-start | bytes 4718592 | tf_op jit(solution)/shard_map/all_to_all | solution.py:92
  579.0 4.5 fusion.39
  583.5 52.0 %all-to-all-done.2 = bf16[64,16,1152]{2,1,0:T(8,128)(2,1)S(1)} async-done(((bf16[64,16,1152]{2,1,0:T(8,128)(2,1)}), bf16[64,16,1152]{2,1,0:T(8,128)(2,1)S(1)}, u32[]{:S(2)}, u32[]{:S(2)}) %all-to-all-start.2) | async-done | bytes 2359328 | tf_op jit(solution)/shard_map/all_to_all | solution.py:92
  635.6 1.5 convolution_dynamic-update-slice_fusion.15
  637.1 1.5 fusion.10
  642.9 3.0 fusion.26
  (119 shorter events, 13.9 us)
Async XLA Ops:
  6.5 417.0 %copy-start = (bf16[1,4096,384]{2,1,0:T(8,128)(2,1)S(1)}, bf16[1,4096,384]{2,1,0:T(8,128)(2,1)}, u32[]{:S(2)}) copy-start(bf16[1,4096,384]{2,1,0:T(8,128)(2,1)} %param.15) | copy-start | bytes 9437188
  6.5 226.6 %reduce-scatter.3.cloned.1.call-start = ((), (), s32[]{:S(2)}) async-start(), calls=%async_computation.5 | async-start | bytes 1310720 | tf_op jit(solution)/shard_map/reduce_scatter | solution.py:52
  8.7 199.2 %copy-start.22 = (bf16[128,1024]{1,0:T(8,128)(2,1)S(1)}, bf16[128,1024]{1,0:T(8,128)(2,1)}, u32[]{:S(2)}) copy-start(bf16[128,1024]{1,0:T(8,128)(2,1)} %param.9) | copy-start | bytes 786436
  211.8 199.7 %all-gather.2.cloned.1.call-start = ((), (), s32[]{:S(2)}) async-start(), calls=%async_computation.6 | async-start | bytes 11796480 | tf_op jit(solution)/shard_map/all_gather | solution.py:75
  241.0 2.3 copy-start.3
  322.0 241.9 %reduce-scatter.5.cloned.1.call-start = ((), (), s32[]{:S(2)}) async-start(), calls=%async_computation.7 | async-start | bytes 11796480 | tf_op jit(solution)/shard_map/reduce_scatter | solution.py:88
  418.5 5.0 copy-start.18
  442.8 16.9 %copy-start.4 = (bf16[1,384,4096]{1,2,0:T(8,128)(2,1)S(1)}, bf16[1,384,4096]{1,2,0:T(8,128)(2,1)}, u32[]{:S(2)}) copy-start(bf16[1,384,4096]{1,2,0:T(8,128)(2,1)} %copy.135) | copy-start | bytes 9437188
  459.6 2.7 copy-start.39
  568.2 10.7 %copy-start.19 = (f32[128,64]{0,1:T(8,128)S(1)}, f32[128,64]{0,1:T(8,128)}, u32[]{:S(2)}) copy-start(f32[128,64]{0,1:T(8,128)} %get-tuple-element.6) | copy-start | bytes 98308
  568.2 10.7 %copy-start.21 = (s32[128,64]{0,1:T(8,128)S(1)}, s32[128,64]{0,1:T(8,128)}, u32[]{:S(2)}) copy-start(s32[128,64]{0,1:T(8,128)} %copy-done.20) | copy-start | bytes 98308
  568.2 10.7 %copy-start.25 = (pred[1024]{0:T(1024)(128)(4,1)S(1)}, pred[1024]{0:T(1024)(128)(4,1)}, u32[]{:S(2)}) copy-start(pred[1024]{0:T(1024)(128)(4,1)} %get-tuple-element.64) | copy-start | bytes 3076
  568.2 10.7 %copy-start.27 = (pred[1024]{0:T(1024)(128)(4,1)S(1)}, pred[1024]{0:T(1024)(128)(4,1)}, u32[]{:S(2)}) copy-start(pred[1024]{0:T(1024)(128)(4,1)} %get-tuple-element.65) | copy-start | bytes 3076
  568.2 10.7 %copy-start.29 = (pred[1024]{0:T(1024)(128)(4,1)S(1)}, pred[1024]{0:T(1024)(128)(4,1)}, u32[]{:S(2)}) copy-start(pred[1024]{0:T(1024)(128)(4,1)} %get-tuple-element.66) | copy-start | bytes 3076
  568.2 10.7 %copy-start.31 = (pred[1024]{0:T(1024)(128)(4,1)S(1)}, pred[1024]{0:T(1024)(128)(4,1)}, u32[]{:S(2)}) copy-start(pred[1024]{0:T(1024)(128)(4,1)} %get-tuple-element.67) | copy-start | bytes 3076
  568.2 10.7 %copy-start.33 = (pred[1024]{0:T(1024)(128)(4,1)S(1)}, pred[1024]{0:T(1024)(128)(4,1)}, u32[]{:S(2)}) copy-start(pred[1024]{0:T(1024)(128)(4,1)} %get-tuple-element.68) | copy-start | bytes 3076
  568.2 10.7 %copy-start.35 = (pred[1024]{0:T(1024)(128)(4,1)S(1)}, pred[1024]{0:T(1024)(128)(4,1)}, u32[]{:S(2)}) copy-start(pred[1024]{0:T(1024)(128)(4,1)} %get-tuple-element.69) | copy-start | bytes 3076
  568.2 10.7 %copy-start.37 = (pred[1024]{0:T(1024)(128)(4,1)S(1)}, pred[1024]{0:T(1024)(128)(4,1)}, u32[]{:S(2)}) copy-start(pred[1024]{0:T(1024)(128)(4,1)} %get-tuple-element.70) | copy-start | bytes 3076
  568.2 67.3 %all-to-all-start.2 = ((bf16[64,16,1152]{2,1,0:T(8,128)(2,1)}), bf16[64,16,1152]{2,1,0:T(8,128)(2,1)S(1)}, u32[]{:S(2)}, u32[]{:S(2)}) async-start(bf16[64,16,1152]{2,1,0:T(8,128)(2,1)} %pad_maximum_fusion.3), calls=%async_computation.4 | async-start | bytes 4718592 | tf_op jit(solution)/shard_map/all_to_all | solution.py:92
  635.5 7.1 %copy-start.2 = (bf16[64,16,1152]{2,1,0:T(8,128)(2,1)}, bf16[64,16,1152]{2,1,0:T(8,128)(2,1)S(1)}, u32[]{:S(2)}) copy-start(bf16[64,16,1152]{2,1,0:T(8,128)(2,1)S(1)} %all-to-all-done.2) | copy-start | bytes 7077892
  635.5 3.0 copy-start.17
  635.5 3.3 copy-start.16
  635.5 3.6 copy-start.15
  637.0 2.4 copy-start.14
  637.0 2.7 copy-start.13
  637.1 3.0 copy-start.12
  638.6 2.3 copy-start.9
  638.9 2.3 copy-start.8
  639.2 2.3 copy-start.7
  639.5 2.3 copy-start.6
  640.6 2.3 copy-start.5
  642.9 3.0 copy-start.1
  (13 other events, 24.2 us)
Sparse Core Ops, SparseCore 0:
  211.9 21.1 reduce-scatter.2
  322.2 89.3 all-gather.1
  471.3 92.5 reduce-scatter.4
